TPU v7x, 256 devices: a whole 4x4x8 slice. The times are simulated.
256 devices in a mesh: dp: 8 (over z_lo, x), ctx: 32 (over z_hi, y, core).
Axes of the slice: x: 4, y: 4, z: 8 (z_hi: 4, z_lo: 2; z = z_hi * 2 + z_lo), core: 2. Of those that a mesh axis runs over, the one named last changes fastest.
Arguments:
- tokens: bfloat16 [8, 4096, 4096], P('dp', 'ctx'), may hold values from -6 to 6
- proj_weight: bfloat16 [4096, 512], P('dp'), may hold values from -0.09375 to 0.09375
- values: bfloat16 [8, 4096, 2048], P('dp', 'ctx'), may hold values from -60 to 60
- grad_out: bfloat16 [8, 4096, 2048], P('dp', 'ctx'), may hold values from -6 to 6
Outputs:
- attended: bfloat16 [8, 4096, 2048], P('dp', 'ctx')
- grad_tokens: bfloat16 [8, 4096, 4096], P('dp', 'ctx')
- grad_values: bfloat16 [8, 4096, 2048], P('dp', 'ctx')
- grad_proj: float32 [4096, 512], P(('dp', 'ctx'))
All inputs are finite; a program needn't handle non-finite values.
Results may differ from a plain program's by a relative error of at most 0.0049.
Values may be sent and summed in bfloat16 or wider, within the bound.
A program may use at most 192 MiB of HBM per device.

v0:
```python
import jax
import jax.numpy as jnp
from jax import lax
from jax.sharding import PartitionSpec as P

H = 16
F = 16
DH = 128
HIGHEST = lax.Precision.HIGHEST
QUAD_SCALE = 0.17677669529663687
EPSILON = 1e-05


def features(inputs):
    count_heads, count_rows, count_feat = inputs.shape
    linear = jnp.swapaxes(inputs, 1, 2) * 0.5
    square = (inputs[:, :, :, None] * inputs[:, :, None, :]).reshape(
        count_heads, count_rows, count_feat * count_feat
    )
    square = jnp.swapaxes(square, 1, 2) * QUAD_SCALE
    constant_row = jnp.ones((count_heads, 1, count_rows), inputs.dtype)
    return jnp.concatenate([constant_row, linear, square], axis=1)


def block_kernel(query_part, key_part):
    count_rows = query_part.shape[1]
    causal = lax.broadcasted_iota(jnp.int32, (count_rows, count_rows), 0) >= lax.broadcasted_iota(
        jnp.int32, (count_rows, count_rows), 1
    )
    scores = jnp.einsum("htf,hsf->hts", query_part, key_part, precision=HIGHEST) * 0.25
    kernel = jnp.where(causal, 1.0 + scores + 0.5 * scores * scores, 0.0)
    return (causal, scores, kernel)


def normalize(numerator):
    inv_rms = lax.rsqrt(jnp.mean(numerator * numerator, axis=-1, keepdims=True) + EPSILON)
    return (inv_rms, numerator * inv_rms)


def grad_normalize(inv_rms, normed, upstream):
    return inv_rms * (upstream - normed * jnp.mean(normed * upstream, axis=-1, keepdims=True))


def local_backward(
    query_part,
    key_part,
    value_part,
    grad_num,
    causal,
    scores,
    kernel,
    pull_query,
    pull_key,
    feat_key,
    prefix,
    suffix,
):
    mixing = jnp.where(
        causal, jnp.einsum("htd,hsd->hts", grad_num, value_part, precision=HIGHEST), 0.0
    )
    slope = mixing * (1.0 + scores)
    grad_query = jnp.einsum("hts,hsf->htf", slope, key_part, precision=HIGHEST) * 0.25
    grad_key = jnp.einsum("hts,htf->hsf", slope, query_part, precision=HIGHEST) * 0.25
    grad_query = (
        grad_query + pull_query(jnp.einsum("hed,htd->het", prefix, grad_num, precision=HIGHEST))[0]
    )
    grad_key = (
        grad_key + pull_key(jnp.einsum("hed,htd->het", suffix, value_part, precision=HIGHEST))[0]
    )
    grad_value = jnp.einsum("hts,htd->hsd", kernel, grad_num, precision=HIGHEST)
    grad_value = grad_value + jnp.einsum("het,hed->htd", feat_key, suffix, precision=HIGHEST)
    return (grad_query, grad_key, grad_value)


def exclusive(blocks, later):
    count = blocks.shape[0]
    row = lax.broadcasted_iota(jnp.int32, (count, count), 0)
    col = lax.broadcasted_iota(jnp.int32, (count, count), 1)
    chosen = col > row if later else col < row
    return jnp.dot(chosen.astype(jnp.float32), blocks, precision=HIGHEST)


def split_heads(matrix, size):
    return jnp.swapaxes(matrix.reshape(matrix.shape[0], -1, size), 0, 1)


def merge_heads(blocked):
    return jnp.swapaxes(blocked, 0, 1).reshape(blocked.shape[1], -1)


def local(tokens, proj_weight, values, grad_out):
    token_rows = tokens[0]
    query_cols = H * F
    tokens_cols = lax.all_to_all(token_rows, "dp", split_axis=1, concat_axis=0, tiled=True)
    projected = jnp.dot(
        token_rows,
        lax.all_gather(proj_weight, "dp", axis=0, tiled=True),
        preferred_element_type=jnp.float32,
    )
    query_part = split_heads(projected[:, :query_cols], F)
    key_part = split_heads(projected[:, query_cols:], F)
    value_part = split_heads(values[0].astype(jnp.float32), DH)
    upstream = split_heads(grad_out[0].astype(jnp.float32), DH)
    feat_query, pull_query = jax.vjp(features, query_part)
    feat_key, pull_key = jax.vjp(features, key_part)
    local_term = jnp.einsum("het,htd->hed", feat_key, value_part, precision=HIGHEST)
    columns_in = lax.all_to_all(
        local_term.reshape(1, -1), "ctx", split_axis=1, concat_axis=0, tiled=True
    )
    running = exclusive(columns_in, False)
    prefix = lax.all_to_all(running, "ctx", split_axis=0, concat_axis=1, tiled=True).reshape(
        local_term.shape
    )
    causal, scores, kernel = block_kernel(query_part, key_part)
    numerator = jnp.einsum("hts,hsd->htd", kernel, value_part, precision=HIGHEST)
    numerator = numerator + jnp.einsum("het,hed->htd", feat_query, prefix, precision=HIGHEST)
    inv_rms, normed = normalize(numerator)
    attended = merge_heads(normed).astype(jnp.bfloat16)
    grad_num = grad_normalize(inv_rms, normed, upstream)
    carried = jnp.einsum("het,htd->hed", feat_query, grad_num, precision=HIGHEST)
    later_in = lax.all_to_all(
        carried.reshape(1, -1), "ctx", split_axis=1, concat_axis=0, tiled=True
    )
    later_running = exclusive(later_in, True)
    suffix = lax.all_to_all(later_running, "ctx", split_axis=0, concat_axis=1, tiled=True).reshape(
        carried.shape
    )
    grad_query, grad_key, grad_value = local_backward(
        query_part,
        key_part,
        value_part,
        grad_num,
        causal,
        scores,
        kernel,
        pull_query,
        pull_key,
        feat_key,
        prefix,
        suffix,
    )
    grad_proj_rows = jnp.concatenate(
        [merge_heads(grad_query), merge_heads(grad_key)], axis=1
    ).astype(jnp.bfloat16)
    grad_tokens = lax.dot_general(
        grad_proj_rows,
        lax.all_gather(proj_weight, "dp", axis=0, tiled=True),
        (((1,), (1,)), ((), ())),
        preferred_element_type=jnp.float32,
    ).astype(jnp.bfloat16)
    rows_all = lax.all_gather(grad_proj_rows, "dp", axis=0, tiled=True)
    grad_proj = lax.psum_scatter(
        lax.dot_general(
            tokens_cols, rows_all, (((0,), (0,)), ((), ())), preferred_element_type=jnp.float32
        ),
        "ctx",
        scatter_dimension=0,
        tiled=True,
    )
    grad_values = merge_heads(grad_value).astype(jnp.bfloat16)
    return (attended[None], grad_tokens[None], grad_values[None], grad_proj)


def solution(mesh):
    return jax.shard_map(
        local,
        mesh=mesh,
        in_specs=(P("dp", "ctx", None), P("dp", None), P("dp", "ctx", None), P("dp", "ctx", None)),
        out_specs=(
            P("dp", "ctx", None),
            P("dp", "ctx", None),
            P("dp", "ctx", None),
            P(("dp", "ctx"), None),
        ),
        check_vma=False,
    )
```

profile of v0, /device:TPU:2, one launch (start us, length us, event | category | flops | bytes accessed | tf_op | source)
XLA Modules:
  0.0 523.0 jit_solution(1464538950625554450)
XLA Ops:
  7.2 0.7 all-gather.3.cloned.1.call-update
  7.9 1.1 copy.72
  9.1 56.6 %all-gather.3.cloned.1.call-done = bf16[4096,512]{1,0:T(8,128)(2,1)} async-done(((bf16[512,512]{1,0:T(8,128)(2,1)}), bf16[4096,512]{1,0:T(8,128)(2,1)}) %all-gather.3.cloned.1.call-update) | async-done | bytes 4194320 | tf_op jit(solution)/shard_map/all_gather | solution.py:97
  65.7 3.2 fusion.22
  69.1 0.3 multiply_multiply_fusion
  69.4 1.4 copy-done.1
  70.8 2.1 fusion.6
  72.9 3.7 all_to_all.72
  76.6 65.7 %all_to_all.79 = f32[1,32,17472]{2,0,1:T(1,128)S(1)} all-to-all(f32[1,32,17472]{2,0,1:T(1,128)} %all_to_all.72), channel_id=1, replica_groups=mesh['dp'=8,'ctx'=32] {'ctx'}, dimensions={1} | all-to-all | bytes 4472832 | tf_op jit(solution)/shard_map/all_to_all | solution.py:107
  142.3 1.2 convolution_bitcast_fusion.1
  143.5 3.7 copy.50
  147.2 4.5 all-to-all-start.1
  151.8 1.2 copy.51
  153.1 0.7 multiply_bitcast_fusion.1
  153.8 2.7 fusion.60
  156.5 2.9 multiply_multiply_fusion.1
  159.5 46.6 %all-to-all-done.1 = f32[32,1,17472]{2,1,0:T(1,128)S(1)} async-done(((f32[32,1,17472]{2,1,0:T(1,128)}), f32[32,1,17472]{2,1,0:T(1,128)S(1)}, u32[]{:S(2)}, u32[]{:S(2)}) %all-to-all-start.1) | async-done | bytes 2236448 | tf_op jit(solution)/shard_map/all_to_all | solution.py:111
  206.0 7.3 %reduce = f32[32,17472]{1,0:T(8,128)} reduce(f32[32,1,17472]{2,1,0:T(1,128)S(1)} %all-to-all-done.1, f32[]{:T(128)} %constant.24), dimensions={1}, to_apply=%all_to_all.62.reduce_sub_computation | reduce | bytes 4472836 | tf_op jit(solution)/shard_map/all_to_all | solution.py:111
  213.3 2.4 reshape.143
  215.8 6.9 %fusion.8 = f32[16,128,128]{1,2,0:T(8,128)S(1)} fusion(f32[16,273,128]{2,1,0:T(8,128)S(1)} %reshape.143, f32[16,256,128]{2,1,0:T(8,128)} %bitcast.119, f32[16,16,128]{2,1,0:T(8,128)} %multiply_bitcast_fusion.1, f32[273]{0:T(512)S(1)} %pad.5.clone), kind=kOutput, calls=%fused_computation.21 | convolution fusion | flops 859901952 | bytes 5514308 | tf_op jit(solution)/shard_map/het,hed->htd/dot_general | solution.py:116
  222.8 1.4 multiply_reduce_fusion.5
  224.1 0.7 add_rsqrt_fusion
  224.8 0.2 multiply_reduce_fusion.4
  225.1 0.2 subtract_multiply_fusion
  225.3 1.1 copy-done
  226.4 5.3 %fusion.7 = f32[16,273,128]{2,1,0:T(8,128)} fusion(f32[16,128,128]{1,2,0:T(8,128)S(1)} %subtract_multiply_fusion, f32[16,256,128]{2,1,0:T(8,128)S(1)} %bitcast.120, f32[16,16,128]{2,1,0:T(8,128)S(1)} %copy-done.17, f32[273]{0:T(512)S(1)} %pad.5.clone), kind=kOutput, calls=%fused_computation.20 | convolution fusion | flops 859901952 | bytes 5514308 | tf_op jit(solution)/shard_map/het,htd->hed/dot_general | solution.py:120
  231.7 5.2 all_to_all.73
  236.9 58.5 %all_to_all.80 = f32[1,32,17472]{2,0,1:T(1,128)S(1)} all-to-all(f32[1,32,17472]{2,0,1:T(1,128)} %all_to_all.73), channel_id=1, replica_groups=mesh['dp'=8,'ctx'=32] {'ctx'}, dimensions={1} | all-to-all | bytes 4472832 | tf_op jit(solution)/shard_map/all_to_all | solution.py:121
  295.4 1.2 convolution_bitcast_fusion
  296.6 3.8 copy.56
  300.3 5.8 %all-to-all-start.3 = ((f32[32,1,17472]{2,1,0:T(1,128)}), f32[32,1,17472]{2,1,0:T(1,128)}, u32[]{:S(2)}, u32[]{:S(2)}) async-start(f32[32,1,17472]{2,1,0:T(1,128)} %copy.56), calls=%async_computation.3 | async-start | bytes 4489216 | tf_op jit(solution)/shard_map/all_to_all | solution.py:125
  306.1 2.3 copy.57
  308.4 3.9 fusion.61
  312.3 0.3 slice_multiply_fusion.1
  312.6 0.6 copy-done.13
  313.2 1.0 multiply_reduce_fusion.2
  314.2 0.2 copy-done.3
  314.4 0.1 copy-done.8
  314.5 1.0 fusion.9
  315.6 1.0 copy-done.9
  316.6 1.7 fusion.20
  318.3 40.6 %all-to-all-done.3 = f32[32,1,17472]{2,1,0:T(1,128)} async-done(((f32[32,1,17472]{2,1,0:T(1,128)}), f32[32,1,17472]{2,1,0:T(1,128)}, u32[]{:S(2)}, u32[]{:S(2)}) %all-to-all-start.3) | async-done | bytes 2236448 | tf_op jit(solution)/shard_map/all_to_all | solution.py:125
  358.9 7.7 %all-to-all-start.4 = ((bf16[128,8,512]{0,2,1:T(8,128)(2,1)}), bf16[128,8,512]{0,2,1:T(8,128)(2,1)}, u32[]{:S(2)}, u32[]{:S(2)}) async-start(bf16[128,8,512]{0,2,1:T(8,128)(2,1)} %bitcast.40), calls=%async_computation.4 | async-start | bytes 2097152 | tf_op jit(solution)/shard_map/all_to_all | solution.py:94
  366.6 0.2 all-gather.5.cloned.1.call-start
  366.8 8.4 %reduce.1 = f32[32,17472]{1,0:T(8,128)} reduce(f32[32,1,17472]{2,1,0:T(1,128)} %all-to-all-done.3, f32[]{:T(128)} %constant.24), dimensions={1}, to_apply=%all_to_all.67.reduce_sub_computation | reduce | bytes 4472836 | tf_op jit(solution)/shard_map/all_to_all | solution.py:125
  375.3 2.2 reshape.146
  377.5 3.1 fusion.27
  380.5 0.3 slice_multiply_fusion
  380.8 1.1 multiply_reduce_fusion
  381.9 0.1 copy-done.10
  382.0 1.0 fusion.19
  383.1 0.7 pad_maximum_fusion.6
  383.7 0.3 reduce-scatter.4.cloned.1.call-start
  384.1 2.3 copy.58
  386.3 32.8 %all-gather.5.cloned.1.call-done = bf16[1024,512]{0,1:T(8,128)(2,1)} async-done(((bf16[128,512]{0,1:T(8,128)(2,1)}), bf16[1024,512]{0,1:T(8,128)(2,1)}) %all-gather.5.cloned.1.call-update) | async-done | bytes 1048592 | tf_op jit(solution)/shard_map/all_gather | solution.py:151
  419.1 3.3 convolution_bitcast_fusion.2
  422.4 2.5 copy.68
  424.9 2.2 fusion.21
  427.1 2.0 copy.59
  429.1 7.0 %fusion.5 = f32[16,128,128]{1,2,0:T(8,128)S(1)} fusion(f32[16,273,128]{2,1,0:T(8,128)S(1)} %reshape.146, f32[16,256,128]{2,1,0:T(8,128)} %bitcast.122, f32[16,16,128]{2,1,0:T(8,128)S(1)} %copy-done.16, f32[273]{0:T(512)} %copy-done.21), kind=kOutput, calls=%fused_computation.18 | convolution fusion | flops 859901952 | bytes 5514308 | tf_op jit(solution)/shard_map/het,hed->htd/dot_general | solution.py:71
  436.1 1.4 fusion.10
  437.5 1.0 copy.60
  438.5 4.7 fusion
  443.2 72.8 %reduce-scatter.4.cloned.1.call-done = f32[16,512]{1,0:T(8,128)} async-done(((f32[512,512]{1,0:T(8,128)}), f32[16,512]{1,0:T(8,128)}) %reduce-scatter.4.cloned.1.call-update) | async-done | bytes 32784
  (48 shorter events, 0.5 us)
Async XLA Ops:
  7.2 58.6 %all-gather.3.cloned.1.call-start = ((), (), s32[]{:S(2)}) async-start(), calls=%async_computation.6 | async-start | bytes 4718592 | tf_op jit(solution)/shard_map/all_gather | solution.py:97
  9.1 60.3 %copy-start.6 = (bf16[16,8,16,128]{3,2,1,0:T(8,128)(2,1)}, bf16[16,8,16,128]{3,2,1,0:T(8,128)(2,1)S(1)}, u32[]{:S(2)}) copy-start(bf16[16,8,16,128]{3,2,1,0:T(8,128)(2,1)S(1)} %copy.72) | copy-start | bytes 1572868
  9.1 216.3 %copy-start.21 = (f32[273]{0:T(512)}, f32[273]{0:T(512)S(1)}, u32[]{:S(2)}) copy-start(f32[273]{0:T(512)S(1)} %pad.5.clone) | copy-start | bytes 3280
  69.1 3.8 copy-start.15
  69.4 1.4 copy-start.1
  147.2 4.6 copy-start.20
  147.2 58.8 %all-to-all-start.1 = ((f32[32,1,17472]{2,1,0:T(1,128)}), f32[32,1,17472]{2,1,0:T(1,128)S(1)}, u32[]{:S(2)}, u32[]{:S(2)}) async-start(f32[32,1,17472]{2,1,0:T(1,128)} %copy.50), calls=%async_computation.1 | async-start | bytes 4489216 | tf_op jit(solution)/shard_map/all_to_all | solution.py:111
  153.1 0.7 copy-start.12
  156.5 66.2 %copy-start.2 = (f32[16,128,128]{2,1,0:T(8,128)}, f32[16,128,128]{2,1,0:T(8,128)S(1)}, u32[]{:S(2)}) copy-start(f32[16,128,128]{2,1,0:T(8,128)S(1)} %fusion.60) | copy-start | bytes 3145732
  215.8 7.0 %copy-start.7 = (bf16[16,8,16,128]{3,2,1,0:T(8,128)(2,1)S(1)}, bf16[16,8,16,128]{3,2,1,0:T(8,128)(2,1)}, u32[]{:S(2)}) copy-start(bf16[16,8,16,128]{3,2,1,0:T(8,128)(2,1)} %copy-done.6) | copy-start | bytes 1572868
  222.7 2.1 copy-start.11
  224.1 1.0 copy-start.5
  224.8 1.6 copy-start
  224.8 1.6 copy-start.17
  300.3 58.6 %all-to-all-start.3 = ((f32[32,1,17472]{2,1,0:T(1,128)}), f32[32,1,17472]{2,1,0:T(1,128)}, u32[]{:S(2)}, u32[]{:S(2)}) async-start(f32[32,1,17472]{2,1,0:T(1,128)} %copy.56), calls=%async_computation.3 | async-start | bytes 4489216 | tf_op jit(solution)/shard_map/all_to_all | solution.py:125
  312.3 0.9 copy-start.13
  313.2 1.2 copy-start.3
  313.2 1.4 copy-start.8
  315.6 1.0 copy-start.9
  358.9 25.1 %all-to-all-start.4 = ((bf16[128,8,512]{0,2,1:T(8,128)(2,1)}), bf16[128,8,512]{0,2,1:T(8,128)(2,1)}, u32[]{:S(2)}, u32[]{:S(2)}) async-start(bf16[128,8,512]{0,2,1:T(8,128)(2,1)} %bitcast.40), calls=%async_computation.4 | async-start | bytes 2097152 | tf_op jit(solution)/shard_map/all_to_all | solution.py:94
  366.6 52.5 %all-gather.5.cloned.1.call-start = ((), (), s32[]{:S(2)}) async-start(), calls=%async_computation.7 | async-start | bytes 1179648 | tf_op jit(solution)/shard_map/all_gather | solution.py:151
  380.8 1.2 copy-start.10
  380.8 1.2 copy-start.14
  383.0 39.3 %copy-start.18 = (bf16[128,16,16]{0,2,1:T(8,128)(2,1)}, bf16[128,16,16]{0,2,1:T(8,128)(2,1)S(1)}, u32[]{:S(2)}) copy-start(bf16[128,16,16]{0,2,1:T(8,128)(2,1)S(1)} %fusion.19) | copy-start | bytes 196612
  383.7 132.2 %reduce-scatter.4.cloned.1.call-start = ((), (), s32[]{:S(2)}) async-start(), calls=%async_computation.8 | async-start | bytes 1081344
  424.9 4.2 copy-start.16
  429.1 7.0 %copy-start.4 = (f32[16,128,128]{2,1,0:T(8,128)S(1)}, f32[16,128,128]{2,1,0:T(8,128)}, u32[]{:S(2)}) copy-start(f32[16,128,128]{2,1,0:T(8,128)} %copy-done.2) | copy-start | bytes 3145732
  436.1 2.4 copy-start.19
Sparse Core Ops, SparseCore 0:
  9.8 55.8 all-gather.2
  383.9 35.1 all-gather.4
  425.0 90.9 reduce-scatter.3
where the time goes:
time: 531 us; the launch traced here: 523 us
  waiting for transfers between devices  250 us (47%)
  blocking collectives  124 us (23%)
  matrix products  50.9 us (10%)
  local copies, waits for them, and re-layouts  38.5 us (7%)
  other arithmetic  26.1 us (5%)
  starting transfers between devices  18.6 us (4%)
  between operations  14.6 us (3%)
    unnamed x4, waiting for transfers between devices  73.5 us
    all_to_all x1, blocking collectives, local(): lax.all_to_all(local_term.reshape(1, -1), 'ctx', split_axis=1, concat_axi...  65.7 us
    all_to_all x1, blocking collectives, local(): lax.all_to_all(carried.reshape(1, -1), 'ctx', split_axis=1, concat_axis=0...  58.5 us
    all_gather x1, waiting for transfers between devices, local(): lax.all_gather(proj_weight, 'dp', axis=0, tiled=True)  56.6 us
    all_to_all x1, waiting for transfers between devices, local(): lax.all_to_all(running, 'ctx', split_axis=0, concat_axis=1, tiled=True)  46.6 us
    all_to_all x1, waiting for transfers between devices, local(): lax.all_to_all(later_running, 'ctx', split_axis=0, concat_axis=1, tiled=T...  40.6 us
    all_gather x1, waiting for transfers between devices, local(): rows_all = lax.all_gather(grad_proj_rows, 'dp', axis=0, tiled=True)  32.8 us
    unnamed x49, local copies, waits for them, and re-layouts  13.7 us
  transfers between devices with their start and end apart: 6, of which 5 were waited for; matrix products, arithmetic and copies ran while one was open for 11% of the time, Pallas kernels for 0%

commit v1 on v0

--- a/solution.py
+++ b/solution.py
@@ -9,6 +9,11 @@
 HIGHEST = lax.Precision.HIGHEST
 QUAD_SCALE = 0.17677669529663687
 EPSILON = 1e-05
+
+
+def swapped_in(x, mesh_axis, dim):
+    sent = jnp.stack([x] * lax.axis_size(mesh_axis))
+    return jnp.concatenate(lax.all_to_all(sent, mesh_axis, 0, 0), axis=dim)
 
 
 def features(inputs):
@@ -93,9 +98,7 @@
     query_cols = H * F
     tokens_cols = lax.all_to_all(token_rows, "dp", split_axis=1, concat_axis=0, tiled=True)
     projected = jnp.dot(
-        token_rows,
-        lax.all_gather(proj_weight, "dp", axis=0, tiled=True),
-        preferred_element_type=jnp.float32,
+        token_rows, swapped_in(proj_weight, "dp", 0), preferred_element_type=jnp.float32
     )
     query_part = split_heads(projected[:, :query_cols], F)
     key_part = split_heads(projected[:, query_cols:], F)

time: 531 us -> 583 us (1.098)
  blocking collectives: 124 us -> 166 us
  waiting for transfers between devices: 250 us -> 260 us
    all_to_all x1, waiting for transfers between devices: 0.01 us -> 46.8 us  [swapped_in(): return jnp.concatenate(lax.all_to_all(sent, mesh_axis, 0, 0), axis=dim)]
    all_to_all x0 -> x1, blocking collectives: none -> 28 us  [local(): lax.all_to_all(token_rows, 'dp', split_axis=1, concat_axis=0, tiled=True)]
    all_gather x1, waiting for transfers between devices: 56.6 us -> 32.6 us  [local(): lax.all_gather(proj_weight, 'dp', axis=0, tiled=True)]
    unnamed x4, waiting for transfers between devices: 73.5 us -> 90.5 us
    all_gather x1, waiting for transfers between devices: 32.8 us -> 17.1 us  [local(): rows_all = lax.all_gather(grad_proj_rows, 'dp', axis=0, tiled=True)]
    all_to_all x1, blocking collectives: 58.5 us -> 72.6 us  [local(): lax.all_to_all(carried.reshape(1, -1), 'ctx', split_axis=1, concat_axis=0...]
    all_to_all x1, waiting for transfers between devices: 46.6 us -> 34.1 us  [local(): lax.all_to_all(running, 'ctx', split_axis=0, concat_axis=1, tiled=True)]
    unnamed x49 -> x53, local copies, waits for them, and re-layouts: 13.7 us -> 12.7 us
  transfers between devices with their start and end apart: 6 -> 6, of which waited for: 5 -> 6; matrix products, arithmetic and copies ran while one was open for 11% -> 8% of each run, Pallas kernels for 0% -> 0%
where the time goes in v1:
time: 583 us; the launch traced here: 575 us
  waiting for transfers between devices  260 us (45%)
  blocking collectives  166 us (28%)
  matrix products  50.6 us (9%)
  local copies, waits for them, and re-layouts  40.7 us (7%)
  other arithmetic  26.4 us (5%)
  starting transfers between devices  16.9 us (3%)
  between operations  14.5 us (2%)
    unnamed x4, waiting for transfers between devices  90.5 us
    all_to_all x1, blocking collectives, local(): lax.all_to_all(carried.reshape(1, -1), 'ctx', split_axis=1, concat_axis=0...  72.6 us
    all_to_all x1, blocking collectives, local(): lax.all_to_all(local_term.reshape(1, -1), 'ctx', split_axis=1, concat_axi...  65.4 us
    all_to_all x1, waiting for transfers between devices, swapped_in(): return jnp.concatenate(lax.all_to_all(sent, mesh_axis, 0, 0), axis=dim)  46.8 us
    all_to_all x1, waiting for transfers between devices, local(): lax.all_to_all(later_running, 'ctx', split_axis=0, concat_axis=1, tiled=T...  38.9 us
    all_to_all x1, waiting for transfers between devices, local(): lax.all_to_all(running, 'ctx', split_axis=0, concat_axis=1, tiled=True)  34.1 us
    all_gather x1, waiting for transfers between devices, local(): lax.all_gather(proj_weight, 'dp', axis=0, tiled=True)  32.6 us
    all_to_all x1, blocking collectives, local(): lax.all_to_all(token_rows, 'dp', split_axis=1, concat_axis=0, tiled=True)  28 us
  transfers between devices with their start and end apart: 6, of which 6 were waited for; matrix products, arithmetic and copies ran while one was open for 8% of the time, Pallas kernels for 0%

profile of v1, /device:TPU:2, one launch (start us, length us, event | category | flops | bytes accessed | tf_op | source)
XLA Modules:
  0.0 575.1 jit_solution(857788739389551473)
XLA Ops:
  7.2 3.4 stack.2
  10.6 6.8 %all-to-all-start = ((bf16[8,512,512]{2,1,0:T(8,128)(2,1)}), bf16[8,512,512]{2,1,0:T(8,128)(2,1)}, u32[]{:S(2)}, u32[]{:S(2)}) async-start(bf16[8,512,512]{2,1,0:T(8,128)(2,1)} %stack.2), calls=%async_computation | async-start | bytes 8388608 | tf_op jit(solution)/shard_map/all_to_all | solution.py:16
  17.5 46.8 %all-to-all-done = bf16[8,512,512]{2,1,0:T(8,128)(2,1)} async-done(((bf16[8,512,512]{2,1,0:T(8,128)(2,1)}), bf16[8,512,512]{2,1,0:T(8,128)(2,1)}, u32[]{:S(2)}, u32[]{:S(2)}) %all-to-all-start) | async-done | bytes 4194336 | tf_op jit(solution)/shard_map/all_to_all | solution.py:16
  64.3 2.9 fusion.22
  67.4 0.3 multiply_multiply_fusion
  67.7 1.3 copy-done.1
  69.0 2.1 fusion.6
  71.1 3.7 all_to_all.76
  74.8 65.4 %all_to_all.84 = f32[1,32,17472]{2,0,1:T(1,128)S(1)} all-to-all(f32[1,32,17472]{2,0,1:T(1,128)} %all_to_all.76), channel_id=1, replica_groups=mesh['dp'=8,'ctx'=32] {'ctx'}, dimensions={1} | all-to-all | bytes 4472832 | tf_op jit(solution)/shard_map/all_to_all | solution.py:110
  140.2 1.2 convolution_bitcast_fusion.1
  141.4 3.8 copy.50
  145.1 5.1 all-to-all-start.2
  150.2 1.2 copy.51
  151.5 0.7 multiply_bitcast_fusion.1
  152.2 2.7 fusion.60
  154.9 2.9 multiply_multiply_fusion.1
  157.9 34.1 %all-to-all-done.2 = f32[32,1,17472]{2,1,0:T(1,128)S(1)} async-done(((f32[32,1,17472]{2,1,0:T(1,128)}), f32[32,1,17472]{2,1,0:T(1,128)S(1)}, u32[]{:S(2)}, u32[]{:S(2)}) %all-to-all-start.2) | async-done | bytes 2236448 | tf_op jit(solution)/shard_map/all_to_all | solution.py:114
  191.9 7.4 %reduce = f32[32,17472]{1,0:T(8,128)} reduce(f32[32,1,17472]{2,1,0:T(1,128)S(1)} %all-to-all-done.2, f32[]{:T(128)} %constant.24), dimensions={1}, to_apply=%all_to_all.66.reduce_sub_computation | reduce | bytes 4472836 | tf_op jit(solution)/shard_map/all_to_all | solution.py:114
  199.3 2.7 reshape.149
  202.0 6.9 %fusion.8 = f32[16,128,128]{1,2,0:T(8,128)S(1)} fusion(f32[16,273,128]{2,1,0:T(8,128)S(1)} %reshape.149, f32[16,256,128]{2,1,0:T(8,128)} %bitcast.120, f32[16,16,128]{2,1,0:T(8,128)} %multiply_bitcast_fusion.1, f32[273]{0:T(512)S(1)} %pad.5.clone), kind=kOutput, calls=%fused_computation.21 | convolution fusion | flops 859901952 | bytes 5514308 | tf_op jit(solution)/shard_map/het,hed->htd/dot_general | solution.py:119
  209.0 1.4 multiply_reduce_fusion.5
  210.3 0.6 add_rsqrt_fusion
  211.0 0.2 multiply_reduce_fusion.4
  211.3 0.2 subtract_multiply_fusion
  211.5 1.0 copy-done
  212.6 5.3 fusion.7
  217.9 4.9 all_to_all.77
  222.8 72.6 %all_to_all.85 = f32[1,32,17472]{2,0,1:T(1,128)S(1)} all-to-all(f32[1,32,17472]{2,0,1:T(1,128)} %all_to_all.77), channel_id=1, replica_groups=mesh['dp'=8,'ctx'=32] {'ctx'}, dimensions={1} | all-to-all | bytes 4472832 | tf_op jit(solution)/shard_map/all_to_all | solution.py:124
  295.4 1.2 convolution_bitcast_fusion
  296.6 3.7 copy.56
  300.3 4.9 all-to-all-start.4
  305.2 3.9 fusion.61
  309.1 0.3 slice_multiply_fusion.1
  309.4 0.6 copy-done.13
  310.0 1.0 multiply_reduce_fusion.2
  311.0 0.2 copy-done.3
  311.2 0.1 copy-done.8
  311.4 1.0 fusion.9
  312.4 0.9 copy-done.10
  313.3 1.7 fusion.20
  315.1 38.9 %all-to-all-done.4 = f32[32,1,17472]{2,1,0:T(1,128)} async-done(((f32[32,1,17472]{2,1,0:T(1,128)}), f32[32,1,17472]{2,1,0:T(1,128)}, u32[]{:S(2)}, u32[]{:S(2)}) %all-to-all-start.4) | async-done | bytes 2236448 | tf_op jit(solution)/shard_map/all_to_all | solution.py:128
  354.0 8.6 %reduce.1 = f32[32,17472]{1,0:T(8,128)} reduce(f32[32,1,17472]{2,1,0:T(1,128)} %all-to-all-done.4, f32[]{:T(128)} %constant.24), dimensions={1}, to_apply=%all_to_all.71.reduce_sub_computation | reduce | bytes 4472836 | tf_op jit(solution)/shard_map/all_to_all | solution.py:128
  362.6 2.2 reshape.152
  364.8 3.1 fusion.27
  367.9 0.3 slice_multiply_fusion
  368.2 1.1 multiply_reduce_fusion
  369.3 0.1 copy-done.11
  369.4 1.0 fusion.19
  370.4 0.7 pad_maximum_fusion.6
  371.2 0.7 all-gather.3.cloned.1.call-update
  371.9 2.3 copy.57
  374.2 28.0 %all_to_all.86 = bf16[128,8,512]{0,2,1:T(8,128)(2,1)} all-to-all(bf16[128,8,512]{0,2,1:T(8,128)(2,1)} %bitcast.143), channel_id=1, replica_groups=mesh['dp'=8,'ctx'=32] {'dp'}, dimensions={1} | all-to-all | bytes 2097152 | tf_op jit(solution)/shard_map/all_to_all | solution.py:99
  402.2 2.3 copy.58
  404.5 17.1 %all-gather.5.cloned.1.call-done = bf16[1024,512]{0,1:T(8,128)(2,1)} async-done(((bf16[128,512]{0,1:T(8,128)(2,1)}), bf16[1024,512]{0,1:T(8,128)(2,1)}) %all-gather.5.cloned.1.call-update) | async-done | bytes 1048592 | tf_op jit(solution)/shard_map/all_gather | solution.py:154
  421.6 3.3 convolution_bitcast_fusion.2
  424.8 2.6 copy.68
  427.5 2.2 fusion.21
  429.7 2.0 copy.59
  431.7 7.0 %fusion.5 = f32[16,128,128]{1,2,0:T(8,128)S(1)} fusion(f32[16,273,128]{2,1,0:T(8,128)S(1)} %reshape.152, f32[16,256,128]{2,1,0:T(8,128)} %bitcast.123, f32[16,16,128]{2,1,0:T(8,128)S(1)} %copy-done.17, f32[273]{0:T(512)} %copy-done.23), kind=kOutput, calls=%fused_computation.18 | convolution fusion | flops 859901952 | bytes 5514308 | tf_op jit(solution)/shard_map/het,hed->htd/dot_general | solution.py:76
  438.8 1.4 fusion.10
  440.1 1.0 copy.60
  441.1 32.6 %all-gather.3.cloned.1.call-done = bf16[4096,512]{1,0:T(8,128)(2,1)} async-done(((bf16[512,512]{1,0:T(8,128)(2,1)}), bf16[4096,512]{1,0:T(8,128)(2,1)}) %all-gather.3.cloned.1.call-update) | async-done | bytes 4194320 | tf_op jit(solution)/shard_map/all_gather | solution.py:150
  473.8 4.7 fusion
  478.4 89.8 %reduce-scatter.4.cloned.1.call-done = f32[16,512]{1,0:T(8,128)} async-done(((f32[512,512]{1,0:T(8,128)}), f32[16,512]{1,0:T(8,128)}) %reduce-scatter.4.cloned.1.call-update) | async-done | bytes 32784
  (54 shorter events, 0.7 us)
Async XLA Ops:
  10.6 6.8 %copy-start.22 = (bf16[1,128,2048]{2,1,0:T(8,128)(2,1)S(1)}, bf16[1,128,2048]{2,1,0:T(8,128)(2,1)}, u32[]{:S(2)}) copy-start(bf16[1,128,2048]{2,1,0:T(8,128)(2,1)} %param.6) | copy-start | bytes 1572868
  10.6 53.8 %copy-start.15 = (bf16[1,128,4096]{2,1,0:T(8,128)(2,1)S(1)}, bf16[1,128,4096]{2,1,0:T(8,128)(2,1)}, u32[]{:S(2)}) copy-start(bf16[1,128,4096]{2,1,0:T(8,128)(2,1)} %param.4) | copy-start | bytes 3145732
  10.6 53.8 %all-to-all-start = ((bf16[8,512,512]{2,1,0:T(8,128)(2,1)}), bf16[8,512,512]{2,1,0:T(8,128)(2,1)}, u32[]{:S(2)}, u32[]{:S(2)}) async-start(bf16[8,512,512]{2,1,0:T(8,128)(2,1)} %stack.2), calls=%async_computation | async-start | bytes 8388608 | tf_op jit(solution)/shard_map/all_to_all | solution.py:16
  17.5 50.2 %copy-start.6 = (bf16[16,8,16,128]{3,2,1,0:T(8,128)(2,1)}, bf16[16,8,16,128]{3,2,1,0:T(8,128)(2,1)S(1)}, u32[]{:S(2)}) copy-start(bf16[16,8,16,128]{3,2,1,0:T(8,128)(2,1)S(1)} %copy.72) | copy-start | bytes 1572868
  17.5 194.0 %copy-start.23 = (f32[273]{0:T(512)}, f32[273]{0:T(512)S(1)}, u32[]{:S(2)}) copy-start(f32[273]{0:T(512)S(1)} %pad.5.clone) | copy-start | bytes 3280
  67.6 1.3 copy-start.1
  67.7 3.4 copy-start.16
  145.1 5.1 copy-start.21
  145.1 46.8 %all-to-all-start.2 = ((f32[32,1,17472]{2,1,0:T(1,128)}), f32[32,1,17472]{2,1,0:T(1,128)S(1)}, u32[]{:S(2)}, u32[]{:S(2)}) async-start(f32[32,1,17472]{2,1,0:T(1,128)} %copy.50), calls=%async_computation.2 | async-start | bytes 4489216 | tf_op jit(solution)/shard_map/all_to_all | solution.py:114
  151.5 0.7 copy-start.12
  154.9 54.0 %copy-start.2 = (f32[16,128,128]{2,1,0:T(8,128)}, f32[16,128,128]{2,1,0:T(8,128)S(1)}, u32[]{:S(2)}) copy-start(f32[16,128,128]{2,1,0:T(8,128)S(1)} %fusion.60) | copy-start | bytes 3145732
  202.0 7.0 %copy-start.7 = (bf16[16,8,16,128]{3,2,1,0:T(8,128)(2,1)S(1)}, bf16[16,8,16,128]{3,2,1,0:T(8,128)(2,1)}, u32[]{:S(2)}) copy-start(bf16[16,8,16,128]{3,2,1,0:T(8,128)(2,1)} %copy-done.6) | copy-start | bytes 1572868
  208.9 2.1 copy-start.9
  210.3 1.0 copy-start.5
  211.0 1.6 copy-start
  211.0 1.6 copy-start.18
  300.3 53.7 %all-to-all-start.4 = ((f32[32,1,17472]{2,1,0:T(1,128)}), f32[32,1,17472]{2,1,0:T(1,128)}, u32[]{:S(2)}, u32[]{:S(2)}) async-start(f32[32,1,17472]{2,1,0:T(1,128)} %copy.56), calls=%async_computation.4 | async-start | bytes 4489216 | tf_op jit(solution)/shard_map/all_to_all | solution.py:128
  305.2 116.4 %all-gather.5.cloned.1.call-start = ((), (), s32[]{:S(2)}) async-start(), calls=%async_computation.8 | async-start | bytes 1179648 | tf_op jit(solution)/shard_map/all_gather | solution.py:154
  309.1 0.9 copy-start.13
  310.0 1.2 copy-start.3
  310.0 1.4 copy-start.8
  312.4 1.0 copy-start.10
  368.2 1.2 copy-start.11
  368.2 1.2 copy-start.14
  370.4 31.8 %copy-start.19 = (bf16[128,16,16]{0,2,1:T(8,128)(2,1)}, bf16[128,16,16]{0,2,1:T(8,128)(2,1)S(1)}, u32[]{:S(2)}) copy-start(bf16[128,16,16]{0,2,1:T(8,128)(2,1)S(1)} %fusion.19) | copy-start | bytes 196612
  371.1 102.6 %all-gather.3.cloned.1.call-start = ((), (), s32[]{:S(2)}) async-start(), calls=%async_computation.7 | async-start | bytes 4718592 | tf_op jit(solution)/shard_map/all_gather | solution.py:150
  371.9 196.3 %reduce-scatter.4.cloned.1.call-start = ((), (), s32[]{:S(2)}) async-start(), calls=%async_computation.9 | async-start | bytes 1081344
  427.5 4.2 copy-start.17
  431.7 7.0 %copy-start.4 = (f32[16,128,128]{2,1,0:T(8,128)S(1)}, f32[16,128,128]{2,1,0:T(8,128)}, u32[]{:S(2)}) copy-start(f32[16,128,128]{2,1,0:T(8,128)} %copy-done.2) | copy-start | bytes 3145732
  438.8 35.0 %copy-start.20 = (bf16[128,16,16]{0,2,1:T(8,128)(2,1)S(1)}, bf16[128,16,16]{0,2,1:T(8,128)(2,1)}, u32[]{:S(2)}) copy-start(bf16[128,16,16]{0,2,1:T(8,128)(2,1)} %copy-done.19) | copy-start | bytes 196612
Sparse Core Ops, SparseCore 0:
  371.2 50.2 all-gather.4
  423.4 50.3 all-gather.2
  478.1 90.0 reduce-scatter.3
